TPU v7x, 512 devices: a whole 4x4x16 slice. The times are simulated.
512 devices in a mesh: slab: 128 (over z, y, core), mirror: 4 (over x).
Axes of the slice: x: 4, y: 4, z: 16, core: 2. Of those that a mesh axis runs over, the one named last changes fastest.
Arguments:
- a_blocks: bfloat16 [16384, 7, 4096], P(('slab', 'mirror'))
- a_cols: int32 [16384, 7], P(('slab', 'mirror')), may hold values from 0 to 16383, as said below
- p_blocks: bfloat16 [16384, 4096], P(('slab', 'mirror'))
- p_agg: int32 [16384], P(('slab', 'mirror')), may hold values from 0 to 8191, as said below
Outputs:
- coarse_blocks: bfloat16 [8192, 7, 4096], P(('slab', 'mirror'))
- jacobi_inverses: float32 [8192, 4096], P(('slab', 'mirror'))
Inputs may be any that keep to these rules, and one draw needn't show every extreme that they name: `a_cols`: block 0 of row g has column g. Every other column of a row on the device of flattened index s * 4 + m lies on a device of the same slab index and mirror index m - 1, m or m + 1, each device holding 32 consecutive rows. The two fine rows of one aggregate have their k-th columns in one common aggregate. `p_agg`: each aggregate holds exactly two fine rows, at the same mirror index on the two devices whose slab indices differ in the lowest bit; aggregate c belongs to the device of flattened index c // 16, which is one of those two, and each of the two devices owns half of the pair's aggregates.
All inputs are finite; a program needn't handle non-finite values.
Results may differ from a plain program's by a relative error of at most 0.0075.
Values may be sent and summed in bfloat16 or wider, within the bound.
A program may use at most 64 MiB of HBM per device.

v0:
```python
import jax
import jax.numpy as jnp
from jax import lax
from jax.sharding import PartitionSpec as P

BLOCK = 64


def with_halo(array, sides, width):
    for axis, dim in sides:
        devices, length = (lax.axis_size(axis), array.shape[dim])
        up = [(i, (i + 1) % devices) for i in range(devices - 1)]
        down = [(j, i) for i, j in up]
        last = lax.slice_in_dim(array, length - width, length, axis=dim)
        leading = lax.slice_in_dim(array, 0, width, axis=dim)
        before = lax.ppermute(last, axis, up)
        after = lax.ppermute(leading, axis, down)
        array = jnp.concatenate([before, array, after], axis=dim)
    return array


def from_partner(value, axis, apart):
    mask = 2**apart
    pairs = [(source, source ^ mask) for source in range(lax.axis_size(axis))]
    return lax.ppermute(value, axis, pairs)


def invert_block(matrix):
    lower = jnp.linalg.cholesky(matrix)
    ident = jnp.eye(matrix.shape[0], dtype=matrix.dtype)
    return jax.scipy.linalg.cho_solve((lower, True), ident)


def project(tiles, products):
    return jnp.einsum("rji,rkjl->rkil", tiles, products, preferred_element_type=jnp.float32)


def on_device(a_blocks, a_cols, p_blocks, p_agg):
    rows = p_blocks.shape[0]
    kblk = a_blocks.shape[1]
    half = rows // 2
    mirrors = lax.axis_size("mirror")
    slab_index = lax.axis_index("slab")
    device = slab_index * mirrors + lax.axis_index("mirror")
    window = with_halo(p_blocks, (("mirror", 0),), rows)
    first = (device - 1) * rows
    local = a_cols - first
    remote = jnp.take(window, local.reshape(-1), axis=0).reshape(rows, kblk, BLOCK, BLOCK)
    blocks = a_blocks.reshape(rows, kblk, BLOCK, BLOCK)
    product = jnp.einsum(
        "rkij,rkjl->rkil", blocks, remote, preferred_element_type=jnp.float32
    ).astype(jnp.bfloat16)
    owner = p_agg // half
    parity_row = owner // mirrors % 2
    slot_index = p_agg % half + half * parity_row
    own_tiles = p_blocks.reshape(rows, BLOCK, BLOCK)
    product_sorted = jnp.zeros_like(product).at[slot_index].set(product)
    tiles_sorted = jnp.zeros_like(own_tiles).at[slot_index].set(own_tiles)
    parity_mine = slab_index % 2
    keep_at = parity_mine * half
    send_at = (1 - parity_mine) * half
    kept = project(
        lax.dynamic_slice_in_dim(tiles_sorted, keep_at, half, 0),
        lax.dynamic_slice_in_dim(product_sorted, keep_at, half, 0),
    )
    outgoing = project(
        lax.dynamic_slice_in_dim(tiles_sorted, send_at, half, 0),
        lax.dynamic_slice_in_dim(product_sorted, send_at, half, 0),
    )
    arrived = from_partner(
        outgoing.reshape(half, kblk, BLOCK * BLOCK).astype(jnp.bfloat16), "slab", 0
    ).astype(jnp.float32)
    total = kept + arrived.reshape(half, kblk, BLOCK, BLOCK)
    coarse_blocks = total.reshape(half, kblk, BLOCK * BLOCK).astype(jnp.bfloat16)
    diagonal = total[:, 0]
    symmetric = 0.5 * (diagonal + jnp.swapaxes(diagonal, 1, 2))
    jacobi_inverses = jax.vmap(invert_block)(symmetric).reshape(half, BLOCK * BLOCK)
    return (coarse_blocks, jacobi_inverses)


def solution(mesh):
    placed = (
        P(("slab", "mirror"), None, None),
        P(("slab", "mirror"), None),
        P(("slab", "mirror"), None),
        P(("slab", "mirror")),
    )
    return jax.shard_map(
        on_device,
        mesh=mesh,
        in_specs=placed,
        out_specs=(P(("slab", "mirror"), None, None), P(("slab", "mirror"), None)),
        check_vma=False,
    )
```

profile of v0, /device:TPU:1, one launch (start us, length us, event | category | flops | bytes accessed | tf_op | source)
XLA Modules:
  0.0 271.2 jit_solution(16753926579965403564)
XLA Ops:
  0.6 4.0 %collective-permute-start = (bf16[32,4096]{1,0:T(8,128)(2,1)}, bf16[32,4096]{1,0:T(8,128)(2,1)S(1)}, u32[]{:S(2)}, u32[]{:S(2)}) collective-permute-start(bf16[32,4096]{1,0:T(8,128)(2,1)} %param.6), channel_id=1, source_target_pairs={{0,1},{1,2},{2,3},{4,5},{5,6},{6,7},{8,9},{9,10},{10,11},{12,13},{... | collective-permute-start | bytes 786440 | tf_op jit(solution)/shard_map/ppermute | solution.py:16
  4.6 1.3 collective-permute-start.1
  5.9 1.5 reshape.108
  7.4 0.7 compare_and_fusion
  8.4 6.3 %reshape.81 = bf16[32,7,64,64]{3,2,0,1:T(8,128)(2,1)} reshape(bf16[32,7,4096]{2,0,1:T(8,128)(2,1)} %param.4) | data formatting | bytes 3670016 | tf_op jit(solution)/shard_map/reshape | solution.py:49
  14.9 1.6 scatter_fusion.1
  16.6 1.7 gather_fusion
  18.3 5.0 %gather.7 = bf16[32,7,64,64]{3,2,1,0:T(8,128)(2,1)} reshape(bf16[224,4096]{1,0:T(8,128)(2,1)S(1)} %gather_fusion) | data formatting | bytes 3670016 | tf_op jit(solution)/shard_map/jit(_take)/gather | solution.py:48
  23.3 6.0 %copy.30 = bf16[32,7,64,64]{2,3,1,0:T(8,128)(2,1)} copy(bf16[32,7,64,64]{3,2,1,0:T(8,128)(2,1)} %gather.7) | data formatting | bytes 3670016 | tf_op jit(solution)/shard_map/jit(_take)/gather | solution.py:48
  29.3 7.1 %convert_bitcast_fusion = bf16[32,7,64,64]{2,3,1,0:T(8,128)(2,1)} fusion(bf16[32,7,64,64]{3,2,0,1:T(8,128)(2,1)} %reshape.81, bf16[32,7,64,64]{2,3,1,0:T(8,128)(2,1)} %copy.30, pred[32,7]{1,0:T(8,128)(4,1)S(1)} %copy.28), kind=kOutput, calls=%fused_computation.6 | convolution fusion | flops 119275520 | bytes 5505248 | tf_op jit(solution)/shard_map/rkij,rkjl->rkil/dot_general | solution.py:50
  36.5 6.1 %copy.32 = bf16[32,7,64,64]{3,2,1,0:T(8,128)(2,1)} copy(bf16[32,7,64,64]{2,3,1,0:T(8,128)(2,1)} %convert_bitcast_fusion) | data formatting | bytes 3670016 | tf_op jit(solution)/shard_map/convert_element_type | solution.py:52
  42.5 2.8 %broadcast_in_dim.28 = bf16[32,7,64,64]{3,2,1,0:T(8,128)(2,1)} broadcast(bf16[]{:T(256)} %constant.121.clone.1), dimensions={} | broadcast | bytes 1835010 | tf_op jit(solution)/shard_map/broadcast_in_dim | solution.py:57
  45.3 10.9 %scatter_fusion = bf16[32,7,64,64]{3,2,1,0:T(8,128)(2,1)} fusion(bf16[32,7,64,64]{3,2,1,0:T(8,128)(2,1)} %broadcast_in_dim.28, s32[32]{0:T(128)S(1)} %compare_select_fusion.2, bf16[32,7,64,64]{3,2,1,0:T(8,128)(2,1)} %copy.32), kind=kCustom, calls=%fused_computation.1 | custom fusion | bytes 5505152 | tf_op jit(solution)/shard_map/scatter | solution.py:57
  56.2 2.2 convert_bitcast_fusion.1
  58.4 2.6 copy.35
  61.0 3.0 %convert_element_type.29 = bf16[16,7,4096]{2,0,1:T(8,128)(2,1)S(1)} reshape(bf16[16,7,64,64]{3,2,0,1:T(8,128)(2,1)} %copy.35) | data formatting | bytes 1835008 | tf_op jit(solution)/shard_map/convert_element_type | solution.py:71
  64.0 6.2 %collective-permute-start.2 = (bf16[16,7,4096]{2,0,1:T(8,128)(2,1)S(1)}, bf16[16,7,4096]{2,0,1:T(8,128)(2,1)S(1)}, u32[]{:S(2)}, u32[]{:S(2)}) collective-permute-start(bf16[16,7,4096]{2,0,1:T(8,128)(2,1)S(1)} %convert_element_type.29), channel_id=1, source_target_pairs={{0,4},{4,0},{8,12},{12,8},{16,20},{20,16},{24,28},{28,24},{32,36},... | collective-permute-start | bytes 2752520 | tf_op jit(solution)/shard_map/ppermute | solution.py:25
  70.3 4.0 %fusion.8 = f32[16,7,64,64]{3,2,0,1:T(8,128)} fusion(bf16[32,64,64]{2,1,0:T(8,128)(2,1)S(1)} %scatter_fusion.1, s32[]{:T(128)S(6)} %select_n.72, bf16[32,7,64,64]{3,2,1,0:T(8,128)(2,1)} %scatter_fusion), kind=kOutput, calls=%fused_computation.9 | convolution fusion | flops 58720256 | bytes 3933184 | tf_op jit(solution)/shard_map/rji,rkjl->rkil/dot_general | solution.py:35
  74.3 2.7 reshape.87
  77.0 5.0 %copy.36 = f32[16,7,64,64]{2,3,0,1:T(8,128)} copy(f32[16,7,64,64]{3,2,0,1:T(8,128)} %reshape.87) | data formatting | bytes 3670016 | tf_op jit(solution)/shard_map/reshape | solution.py:73
  82.0 4.1 %fusion.33 = (bf16[16,7,64,64]{2,3,0,1:T(8,128)(2,1)S(1)}, f32[16,7,64,64]{2,3,0,1:T(8,128)S(1)}) fusion(f32[16,7,64,64]{2,3,0,1:T(8,128)} %copy.36, f32[16,7,64,64]{3,2,0,1:T(8,128)} %fusion.8), kind=kLoop, calls=%fused_computation.61 | loop fusion | flops 917504 | bytes 6422528 | tf_op jit(solution)/shard_map/convert_element_type | solution.py:74
  86.1 1.8 copy-done
  87.9 0.2 copy.38
  88.1 1.1 fusion.15
  89.3 0.2 copy.39
  89.5 93.8 %custom-call.11 = f32[16,64,64]{2,1,0:T(8,128)S(1)} custom-call(f32[16,64,64]{2,1,0:T(8,128)S(1)} %fusion.20), custom_call_target="Cholesky" | custom-call | tf_op jit(solution)/shard_map/vmap(jit(cholesky))/cholesky | solution.py:29
  183.7 78.6 %custom-call.12 = f32[16,1,64,64]{2,3,1,0:T(8,128)S(1)} custom-call(f32[16,1,64,64]{3,2,1,0:T(8,128)S(1)} %select_bitcast_fusion), custom_call_target="InvertDiagBlocksLowerTriangular" | custom-call | tf_op jit(solution)/shard_map/vmap(jit(_cho_solve))/triangular_solve | solution.py:31
  262.3 1.0 fusion.18
  263.3 0.7 fusion.16
  264.0 0.9 reshape.85
  264.9 2.5 copy.37
  267.4 3.8 %convert_element_type.31 = bf16[16,7,4096]{2,0,1:T(8,128)(2,1)} reshape(bf16[16,7,64,64]{3,2,0,1:T(8,128)(2,1)} %copy.37) | data formatting | bytes 1835008 | tf_op jit(solution)/shard_map/convert_element_type | solution.py:74
  (24 shorter events, 1.0 us)
Async XLA Ops:
  0.6 14.1 %copy-start.2 = (s32[32]{0:T(128)S(1)}, s32[32]{0:T(128)}, u32[]{:S(2)}) copy-start(s32[32]{0:T(128)} %param.7) | copy-start | bytes 388
  0.6 15.9 %collective-permute-start = (bf16[32,4096]{1,0:T(8,128)(2,1)}, bf16[32,4096]{1,0:T(8,128)(2,1)S(1)}, u32[]{:S(2)}, u32[]{:S(2)}) collective-permute-start(bf16[32,4096]{1,0:T(8,128)(2,1)} %param.6), channel_id=1, source_target_pairs={{0,1},{1,2},{2,3},{4,5},{5,6},{6,7},{8,9},{9,10},{10,11},{12,13},{... | collective-permute-start | bytes 786440 | tf_op jit(solution)/shard_map/ppermute | solution.py:16
  4.6 11.9 %collective-permute-start.1 = (bf16[32,4096]{1,0:T(8,128)(2,1)}, bf16[32,4096]{1,0:T(8,128)(2,1)S(1)}, u32[]{:S(2)}, u32[]{:S(2)}) collective-permute-start(bf16[32,4096]{1,0:T(8,128)(2,1)} %param.6), channel_id=1, source_target_pairs={{1,0},{2,1},{3,2},{5,4},{6,5},{7,6},{9,8},{10,9},{11,10},{13,12},{... | collective-permute-start | bytes 786440 | tf_op jit(solution)/shard_map/ppermute | solution.py:17
  8.4 8.2 %copy-start.1 = (bf16[32,4096]{1,0:T(8,128)(2,1)S(1)}, bf16[32,4096]{1,0:T(8,128)(2,1)}, u32[]{:S(2)}) copy-start(bf16[32,4096]{1,0:T(8,128)(2,1)} %param.6) | copy-start | bytes 786436
  64.0 10.3 %collective-permute-start.2 = (bf16[16,7,4096]{2,0,1:T(8,128)(2,1)S(1)}, bf16[16,7,4096]{2,0,1:T(8,128)(2,1)S(1)}, u32[]{:S(2)}, u32[]{:S(2)}) collective-permute-start(bf16[16,7,4096]{2,0,1:T(8,128)(2,1)S(1)} %convert_element_type.29), channel_id=1, source_target_pairs={{0,4},{4,0},{8,12},{12,8},{16,20},{20,16},{24,28},{28,24},{32,36},... | collective-permute-start | bytes 2752520 | tf_op jit(solution)/shard_map/ppermute | solution.py:25
  86.1 1.8 copy-start
where the time goes:
time: 272 us; the launch traced here: 271 us
  other arithmetic  179 us (66%)
  local copies, waits for them, and re-layouts  64.9 us (24%)
  matrix products  15 us (6%)
  starting transfers between devices  11.5 us (4%)
    another operation x4, other arithmetic, invert_block(): lower = jnp.linalg.cholesky(matrix)  94 us
    another operation x3, other arithmetic, invert_block(): return jax.scipy.linalg.cho_solve((lower, True), ident)  78.8 us
    gather x3, local copies, waits for them, and re-layouts, on_device(): jnp.take(window, local.reshape(-1), axis=0)  12.7 us
    scatter x1, local copies, waits for them, and re-layouts, on_device(): product_sorted = jnp.zeros_like(product).at[slot_index].set(product)  10.9 us
    reshape x2, local copies, waits for them, and re-layouts, on_device(): total = kept + arrived.reshape(half, kblk, BLOCK, BLOCK)  7.69 us
    dot_general x1, matrix products, on_device(): jnp.einsum('rkij,rkjl->rkil', blocks, remote, preferred_element_type=jnp....  7.15 us
    reshape x1, local copies, waits for them, and re-layouts, on_device(): blocks = a_blocks.reshape(rows, kblk, BLOCK, BLOCK)  6.35 us
    convert_element_type x2, local copies, waits for them, and re-layouts, on_device(): total.reshape(half, kblk, BLOCK * BLOCK).astype(jnp.bfloat16)  6.3 us
  transfers between devices with their start and end apart: 3, of which 0 were waited for; matrix products, arithmetic and copies ran while one was open for 5% of the time, Pallas kernels for 0%

commit v1 on v0

v1 whole, which is shorter than its diff:
```python
import jax
import jax.numpy as jnp
from jax import lax
from jax.experimental import pallas as pl
from jax.experimental.pallas import tpu as pltpu
from jax.sharding import PartitionSpec as P

F32, BF16 = jnp.float32, jnp.bfloat16
BLOCK = 64
LANES = 128
ROWS = 32
HALF = ROWS // 2
PAIRS = HALF // 2
KA = 7
TILES = BLOCK * BLOCK // LANES
CHUNKS = 4
MESH = pl.DeviceIdType.MESH


def rotate(value):
    return pltpu.roll(value, BLOCK, 1)


def dot(left, right):
    return lax.dot_general(left, right, (((1,), (0,)), ((), ())), preferred_element_type=F32)


def rows_of(index, count):
    return pl.ds(pl.multiple_of(index * count, count), count)


def blocks_from_rows(flat, blocks, at):
    blocks = blocks.reshape(blocks.shape[0] * TILES, LANES)
    for t in range(TILES):
        tile = flat[:, t * LANES:(t + 1) * LANES].astype(F32)
        blocks[pl.ds(at * TILES + t, ROWS, stride=TILES), :] = tile


def tiles_from_rows(flat, left_tiles, right_tiles, at):
    left = lax.broadcasted_iota(jnp.int32, (ROWS, LANES), 1) < BLOCK
    left_tiles = left_tiles.reshape(left_tiles.shape[0] * BLOCK, LANES)
    right_tiles = right_tiles.reshape(right_tiles.shape[0] * BLOCK, LANES)
    for t in range(TILES):
        tile = flat[:, t * LANES:(t + 1) * LANES].astype(F32)
        turned = rotate(tile)
        even = pl.ds(at * BLOCK + 2 * t, ROWS, stride=BLOCK)
        odd = pl.ds(at * BLOCK + 2 * t + 1, ROWS, stride=BLOCK)
        left_tiles[even, :] = jnp.where(left, tile, 0.0)
        left_tiles[odd, :] = jnp.where(left, turned, 0.0)
        right_tiles[even, :] = jnp.where(left, 0.0, turned)
        right_tiles[odd, :] = jnp.where(left, 0.0, tile)


def transposed_tiles(left_tiles, flipped):
    r = lax.broadcasted_iota(jnp.int32, (BLOCK, LANES), 0)
    c = lax.broadcasted_iota(jnp.int32, (BLOCK, LANES), 1)
    pick = (c == 2 * (r % 32) + r // 32).astype(BF16)
    wide = c < BLOCK
    left_tiles = left_tiles.reshape(left_tiles.shape[0] * BLOCK, LANES)

    def body(p, carry):
        parts = []
        for side in range(2):
            start = pl.multiple_of((ROWS + 2 * p + side) * BLOCK, BLOCK)
            parts.append(left_tiles[pl.ds(start, 32, stride=2), :])
            parts.append(left_tiles[pl.ds(start + 1, 32, stride=2), :])
        stacked = jnp.concatenate(parts, axis=0).astype(BF16)
        both = lax.dot_general(pick, stacked, (((1,), (1,)), ((), ())), preferred_element_type=F32)
        turned = rotate(both)
        flipped[2 * p] = jnp.where(wide, both, turned).astype(BF16)
        flipped[2 * p + 1] = jnp.where(wide, turned, both).astype(BF16)
        return carry

    lax.fori_loop(0, HALF, body, 0)


def pair_flipped(p, table, flipped):
    wide = lax.broadcasted_iota(jnp.int32, (BLOCK, LANES), 1) < BLOCK
    one = flipped[table[(2 * p) * 8 + KA]]
    two = flipped[table[(2 * p + 1) * 8 + KA]]
    return jnp.where(wide, one, two)


def pair_terms(p, k, outer, table, blocks, left_tiles, right_tiles):
    left = lax.broadcasted_iota(jnp.int32, (32, LANES), 1) < BLOCK
    wide = lax.broadcasted_iota(jnp.int32, (BLOCK, LANES), 1) < BLOCK
    first, second = 2 * p, 2 * p + 1
    a1 = blocks[k * ROWS + table[first * 8 + KA]]
    a2 = blocks[k * ROWS + table[second * 8 + KA]]
    even = jnp.where(left, a1, rotate(a2))
    odd = jnp.where(left, rotate(a1), a2)
    lhs = jnp.concatenate([even, odd], axis=0).astype(BF16)
    rhs = jnp.concatenate(
        [
            left_tiles[table[first * 8 + k]],
            right_tiles[table[second * 8 + k]],
        ],
        axis=0,
    ).astype(BF16)
    product = dot(lhs, rhs)
    spread = jnp.concatenate(
        [jnp.where(wide, product, 0.0), jnp.where(wide, 0.0, product)], axis=0
    ).astype(BF16)
    return dot(outer, spread)


def split_pair(total):
    left = lax.broadcasted_iota(jnp.int32, (32, LANES), 1) < BLOCK
    even, odd = total[:32], total[32:]
    return jnp.where(left, even, rotate(odd)), jnp.where(left, rotate(even), odd)


def invert_all(v):
    lanes = lax.broadcasted_iota(jnp.int32, (BLOCK, LANES), 1)
    sub = lax.broadcasted_iota(jnp.int32, (BLOCK, LANES), 0)

    def body(tk, carry):
        for inner in range(16):
            h, q = inner % 2, inner // 2
            k = tk * 16 + inner
            index = (lanes // 8) * 8 + q
            slabs = [(2 * tk + h + d) % 8 for d in range(8)]
            cols = [v[pl.ds(s * BLOCK + k, 1), :] for s in slabs]
            row = jnp.take_along_axis(v[rows_of(slabs[0], BLOCK), :], index, axis=1)
            pivot = jnp.take_along_axis(
                jnp.broadcast_to(cols[0], (8, LANES)), index[:8], axis=1
            )[:1]
            inverse = 1.0 / pivot
            here = sub == k
            scaled = jnp.where(here, inverse, row * inverse)
            for d in range(8):
                slab = v[rows_of(slabs[d], BLOCK), :]
                new = jnp.where(here, 0.0, slab) - cols[d] * scaled
                if d == 0:
                    new = jnp.where(lanes % 8 == q, scaled, new)
                v[rows_of(slabs[d], BLOCK), :] = new
        return carry

    lax.fori_loop(0, 4, body, 0)


def kernel(
    table, a_hbm, p_hbm, coarse_ref, inverse_ref,
    a_flat, p_flat, halo, blocks, left_tiles, right_tiles, flipped,
    first_send, first_got, rest_send, rest_got, kept, whole, nat, v,
    a_sem, p_sem, halo_send, halo_recv, first_sem, rest_send_sem, rest_recv_sem,
):
    slab = lax.axis_index("slab")
    mirror = lax.axis_index("mirror")
    mirrors = lax.axis_size("mirror")
    partner = slab + 1 - 2 * (slab % 2)
    up = (mirror + 1) % mirrors
    down = (mirror + mirrors - 1) % mirrors
    others = ({"mirror": up}, {"mirror": down}, {"slab": partner})

    own = pltpu.make_async_copy(p_hbm, p_flat, p_sem)
    own.start()
    loads = [
        pltpu.make_async_copy(a_hbm.at[k], a_flat.at[k], a_sem.at[k]) for k in range(KA)
    ]
    for load in loads:
        load.start()

    barrier = pltpu.get_barrier_semaphore()
    for other in others:
        pl.semaphore_signal(barrier, inc=1, device_id=other, device_id_type=MESH)
    pl.semaphore_wait(barrier, 3)

    halos = [
        pltpu.make_async_remote_copy(
            src_ref=p_hbm, dst_ref=halo.at[side], send_sem=halo_send.at[side],
            recv_sem=halo_recv.at[side], device_id=target, device_id_type=MESH,
        )
        for side, target in enumerate(({"mirror": up}, {"mirror": down}))
    ]
    for copy in halos:
        copy.start()

    own.wait()
    tiles_from_rows(p_flat, left_tiles, right_tiles, ROWS)
    transposed_tiles(left_tiles, flipped)
    loads[0].wait()
    blocks_from_rows(a_flat.at[0], blocks, 0)

    args = (table, blocks, left_tiles, right_tiles)

    def first_out(p, carry):
        outer = pair_flipped(p, table, flipped)
        first_send[rows_of(p, BLOCK), :] = pair_terms(p, 0, outer, *args).astype(BF16)
        return carry

    lax.fori_loop(0, PAIRS, first_out, 0)
    first = pltpu.make_async_remote_copy(
        src_ref=first_send, dst_ref=first_got, send_sem=first_sem.at[0],
        recv_sem=first_sem.at[1], device_id={"slab": partner}, device_id_type=MESH,
    )
    first.start()

    def first_kept(p, carry):
        outer = pair_flipped(p + PAIRS, table, flipped)
        kept[rows_of(p, BLOCK), :] = pair_terms(p + PAIRS, 0, outer, *args)
        return carry

    lax.fori_loop(0, PAIRS, first_kept, 0)

    for k in range(1, KA):
        loads[k].wait()

    def rest_blocks(k, carry):
        blocks_from_rows(a_flat.at[k], blocks, k * ROWS)
        return carry

    lax.fori_loop(1, KA, rest_blocks, 0)

    first.wait()

    wide = lax.broadcasted_iota(jnp.int32, (BLOCK, LANES), 1) < BLOCK

    def diagonal(p, carry):
        total = kept[rows_of(p, BLOCK), :] + first_got[rows_of(p, BLOCK), :].astype(F32)
        one, two = split_pair(total)
        whole[rows_of(2 * p, TILES), :] = one
        whole[rows_of(2 * p + 1, TILES), :] = two
        at = pl.multiple_of(p * BLOCK, BLOCK)
        nat[pl.ds(at, 32, stride=2), :] = total[:32]
        nat[pl.ds(at + 1, 32, stride=2), :] = total[32:]
        plain = nat[rows_of(p, BLOCK), :]
        turned = jnp.concatenate([plain, plain], axis=0).T
        turned = jnp.where(wide, turned[:BLOCK], turned[BLOCK:])
        nat[rows_of(p, BLOCK), :] = 0.5 * (plain + turned)
        even = nat[pl.ds(at, 32, stride=2), :]
        odd = nat[pl.ds(at + 1, 32, stride=2), :]
        one, two = split_pair(jnp.concatenate([even, odd], axis=0))
        kept[rows_of(2 * p, TILES), :] = one
        kept[rows_of(2 * p + 1, TILES), :] = two
        return carry

    lax.fori_loop(0, PAIRS, diagonal, 0)
    for tk in range(4):
        stacked = jnp.concatenate(
            [kept[pl.ds(b * TILES + tk * 8, 8), :] for b in range(HALF)], axis=0
        )
        v[pl.ds(tk * LANES, LANES), :] = stacked.T
    invert_all(v)
    for tk in range(4):
        stacked = v[pl.ds(tk * LANES, LANES), :].T
        for b in range(HALF):
            nat[pl.ds(b * TILES + tk * 8, 8), :] = stacked[b * 8:(b + 1) * 8]
    for t in range(TILES):
        inverse_ref[:, t * LANES:(t + 1) * LANES] = nat[pl.ds(t, HALF, stride=TILES), :]

    for side in range(2):
        halos[side].wait()
        tiles_from_rows(halo.at[side], left_tiles, right_tiles, 2 * side * ROWS)

    per = PAIRS // CHUNKS
    sends = []
    for chunk in range(CHUNKS):
        def rest_out(p, carry):
            outer = pair_flipped(p, table, flipped)
            for k in range(1, KA):
                rest_send[p // per, rows_of((p % per) * (KA - 1) + k - 1, BLOCK), :] = (
                    pair_terms(p, k, outer, *args).astype(BF16)
                )
            return carry

        lax.fori_loop(chunk * per, (chunk + 1) * per, rest_out, 0)
        copy = pltpu.make_async_remote_copy(
            src_ref=rest_send.at[chunk], dst_ref=rest_got.at[chunk],
            send_sem=rest_send_sem.at[chunk], recv_sem=rest_recv_sem.at[chunk],
            device_id={"slab": partner}, device_id_type=MESH,
        )
        copy.start()
        sends.append(copy)

    def rest_kept(p, carry):
        outer = pair_flipped(p + PAIRS, table, flipped)
        for k in range(1, KA):
            kept[rows_of(p * (KA - 1) + k - 1, BLOCK), :] = pair_terms(p + PAIRS, k, outer, *args)
        return carry

    lax.fori_loop(0, PAIRS, rest_kept, 0)
    for chunk in range(CHUNKS):
        sends[chunk].wait()

        def add(p, carry):
            for k in range(1, KA):
                got = rest_got[p // per, rows_of((p % per) * (KA - 1) + k - 1, BLOCK), :]
                total = kept[rows_of(p * (KA - 1) + k - 1, BLOCK), :] + got.astype(F32)
                one, two = split_pair(total)
                whole[rows_of(k * HALF + 2 * p, TILES), :] = one
                whole[rows_of(k * HALF + 2 * p + 1, TILES), :] = two
            return carry

        lax.fori_loop(chunk * per, (chunk + 1) * per, add, 0)

    def flatten(k, carry):
        for t in range(TILES):
            tile = whole[pl.ds(k * HALF * TILES + t, HALF, stride=TILES), :]
            coarse_ref[k, :, t * LANES:(t + 1) * LANES] = tile.astype(BF16)
        return carry

    lax.fori_loop(0, KA, flatten, 0)


def on_device(a_blocks, a_cols, p_blocks, p_agg):
    mirrors = lax.axis_size("mirror")
    slab = lax.axis_index("slab")
    device = slab * mirrors + lax.axis_index("mirror")
    local = a_cols - (device - 1) * ROWS
    mine = ((p_agg // HALF) // mirrors) % 2 == slab % 2
    place = p_agg % HALF + HALF * mine.astype(jnp.int32)
    row = jnp.arange(ROWS, dtype=jnp.int32)
    full = jnp.concatenate([local, row[:, None]], axis=1)
    match = place[None, :] == row[:, None]
    table = jnp.sum(jnp.where(match[:, :, None], full[None], 0), axis=1).reshape(-1)

    vmem = lambda *shape: pltpu.VMEM(shape, F32)
    half = lambda *shape: pltpu.VMEM(shape, BF16)
    dma = pltpu.SemaphoreType.DMA
    coarse, inverse = pl.pallas_call(
        kernel,
        out_shape=(
            jax.ShapeDtypeStruct((KA, HALF, BLOCK * BLOCK), BF16),
            jax.ShapeDtypeStruct((HALF, BLOCK * BLOCK), F32),
        ),
        in_specs=[
            pl.BlockSpec(memory_space=pltpu.SMEM),
            pl.BlockSpec(memory_space=pl.ANY),
            pl.BlockSpec(memory_space=pl.ANY),
        ],
        out_specs=(
            pl.BlockSpec(memory_space=pltpu.VMEM),
            pl.BlockSpec(memory_space=pltpu.VMEM),
        ),
        scratch_shapes=[
            half(KA, ROWS, BLOCK * BLOCK),
            half(ROWS, BLOCK * BLOCK),
            half(2, ROWS, BLOCK * BLOCK),
            vmem(KA * ROWS, TILES, LANES),
            vmem(3 * ROWS, BLOCK, LANES),
            vmem(3 * ROWS, BLOCK, LANES),
            half(ROWS, BLOCK, LANES),
            half(PAIRS * BLOCK, LANES),
            half(PAIRS * BLOCK, LANES),
            half(CHUNKS, PAIRS // CHUNKS * (KA - 1) * BLOCK, LANES),
            half(CHUNKS, PAIRS // CHUNKS * (KA - 1) * BLOCK, LANES),
            vmem(PAIRS * (KA - 1) * BLOCK, LANES),
            vmem(KA * HALF * TILES, LANES),
            vmem(PAIRS * BLOCK, LANES),
            vmem(4 * LANES, LANES),
            dma((KA,)), dma, dma((2,)), dma((2,)), dma((2,)), dma((CHUNKS,)), dma((CHUNKS,)),
        ],
        compiler_params=pltpu.CompilerParams(
            collective_id=0, has_side_effects=True, vmem_limit_bytes=56 * 2**20
        ),
    )(table, jnp.transpose(a_blocks, (1, 0, 2)), p_blocks)
    return jnp.transpose(coarse, (1, 0, 2)), inverse


def solution(mesh):
    placed = (
        P(("slab", "mirror"), None, None),
        P(("slab", "mirror"), None),
        P(("slab", "mirror"), None),
        P(("slab", "mirror")),
    )
    return jax.shard_map(
        on_device,
        mesh=mesh,
        in_specs=placed,
        out_specs=(P(("slab", "mirror"), None, None), P(("slab", "mirror"), None)),
        check_vma=False,
    )
```

time: 272 us -> 51.1 us (0.19)
  other arithmetic: 179 us -> 2.01 us
  local copies, waits for them, and re-layouts: 64.9 us -> 3.58 us
  Pallas kernels: 0 us -> 44.6 us
  matrix products: 15 us -> 0 us
  starting transfers between devices: 11.5 us -> 0 us
    another operation x7 -> x0, other arithmetic: 173 us -> none  [the longest x4 94 us: invert_block(): lower = jnp.linalg.cholesky(matrix)]
    pallas_call x0 -> x1, Pallas kernels: none -> 44.6 us  [on_device(): pl.pallas_call(kernel, out_shape=(jax.ShapeDtypeStruct((KA, HALF, BLOCK *...]
    convert_element_type x5 -> x0, local copies, waits for them, and re-layouts: 18 us -> none  [the longest x2 6.3 us: on_device(): total.reshape(half, kblk, BLOCK * BLOCK).astype(jnp.bfloat16)]
    reshape x6 -> x1, local copies, waits for them, and re-layouts: 16.5 us -> 0.65 us  [on_device(): jnp.sum(jnp.where(match[:, :, None], full[None], 0), axis=1).reshape(-1)]
    dot_general x3 -> x0, matrix products: 13.3 us -> none  [the longest x1 7.15 us: on_device(): jnp.einsum('rkij,rkjl->rkil', blocks, remote, preferred_element_type=jnp....]
    gather x3 -> x0, local copies, waits for them, and re-layouts: 12.7 us -> none  [on_device(): jnp.take(window, local.reshape(-1), axis=0)]
    scatter x2 -> x0, local copies, waits for them, and re-layouts: 12.5 us -> none  [the longest x1 10.9 us: on_device(): product_sorted = jnp.zeros_like(product).at[slot_index].set(product)]
    ppermute x3 -> x0, starting transfers between devices: 11.5 us -> none  [the longest x1 6.24 us: from_partner(): return lax.ppermute(value, axis, pairs)]
  transfers between devices with their start and end apart: 3 -> 0, of which waited for: 0 -> 0; matrix products, arithmetic and copies ran while one was open for 5% -> 0% of each run, Pallas kernels for 0% -> 0%
where the time goes in v1:
time: 51.1 us; the launch traced here: 50.8 us
  Pallas kernels  44.6 us (87%)
  local copies, waits for them, and re-layouts  3.58 us (7%)
  other arithmetic  2.01 us (4%)
  between operations  0.68 us (1%)
    pallas_call x1, Pallas kernels, on_device(): pl.pallas_call(kernel, out_shape=(jax.ShapeDtypeStruct((KA, HALF, BLOCK *...  44.6 us
    unnamed x4, local copies, waits for them, and re-layouts  2.92 us

profile of v1, /device:TPU:1, one launch (start us, length us, event | category | flops | bytes accessed | tf_op | source)
XLA Modules:
  0.0 50.8 jit_solution(6295134626395992679)
XLA Ops:
  0.6 0.7 %fusion = s32[32]{0:T(128)S(1)} fusion(s32[32]{0:T(128)} %param.7, s32[]{:T(128)S(6)} %select_n.33), kind=kLoop, calls=%fused_computation.17 | loop fusion | flops 1536 | bytes 260 | tf_op jit(solution)/shard_map/add | solution.py:312
  1.3 0.7 %broadcast_subtract_fusion = s32[32,7]{0,1:T(8,128)S(1)} fusion(s32[32,7]{0,1:T(8,128)} %param.5, s32[]{:T(128)S(6)} %mul.12), kind=kLoop, calls=%fused_computation.5 | loop fusion | flops 224 | bytes 1796 | tf_op jit(solution)/shard_map/sub | solution.py:310
  2.1 0.6 %select_reduce_fusion = s32[32,8]{1,0:T(8,128)S(1)} fusion(s32[32,8]{0,1:T(8,128)S(1)} %pad_add_fusion, pred[32,32]{1,0:T(8,128)(4,1)S(1)} %iota_compare_fusion), kind=kLoop, calls=%fused_computation | loop fusion | flops 16128 | bytes 3072 | tf_op jit(solution)/shard_map/reduce_sum | solution.py:316
  2.7 0.7 %reshape.26.table = s32[256]{0:T(256)} reshape(s32[32,8]{1,0:T(8,128)S(1)} %select_reduce_fusion) | data formatting | bytes 2048 | tf_op jit(solution)/shard_map/reshape | solution.py:316
  3.3 44.6 %shard_map.59 = (bf16[7,16,4096]{2,1,0:T(8,128)(2,1)}, f32[16,4096]{1,0:T(8,128)}) custom-call(s32[256]{0:T(256)} %reshape.26.table, bf16[7,32,4096]{2,1,0:T(8,128)(2,1)} %bitcast.2, bf16[32,4096]{1,0:T(8,128)(2,1)} %p_hbm.1), custom_call_target="tpu_custom_call" | custom-call | tf_op jit(solution)/shard_map/pallas_call | solution.py:321
  47.9 0.0 copy-start
  47.9 2.2 %copy.10 = bf16[16,7,4096]{2,0,1:T(8,128)(2,1)} copy(bf16[16,7,4096]{2,0,1:T(8,128)(2,1)} %bitcast.3) | data formatting | bytes 1835008
  50.1 0.0 copy-done
  50.1 0.7 %copy.11 = f32[16,4096]{1,0:T(8,128)} copy(f32[16,4096]{1,0:T(8,128)S(1)} %copy-done) | data formatting | bytes 524288
  (3 shorter events, 0.0 us)
Async XLA Ops:
  47.9 2.2 %copy-start = (f32[16,4096]{1,0:T(8,128)S(1)}, f32[16,4096]{1,0:T(8,128)}, u32[]{:S(2)}) copy-start(f32[16,4096]{1,0:T(8,128)} %get-tuple-element.9) | copy-start | bytes 786436

commit v2 on v1

v2 whole, which is shorter than its diff:
```python
import jax
import jax.numpy as jnp
from jax import lax
from jax.experimental import pallas as pl
from jax.experimental.pallas import tpu as pltpu
from jax.sharding import PartitionSpec as P

F32, BF16 = jnp.float32, jnp.bfloat16
BLOCK = 64
LANES = 128
ROWS = 32
HALF = ROWS // 2
PAIRS = HALF // 2
KA = 7
TILES = BLOCK * BLOCK // LANES
CHUNKS = 4
MESH = pl.DeviceIdType.MESH


def rotate(value):
    return pltpu.roll(value, BLOCK, 1)


def dot(left, right):
    return lax.dot_general(left, right, (((1,), (0,)), ((), ())), preferred_element_type=F32)


def rows_of(index, count):
    return pl.ds(pl.multiple_of(index * count, count), count)


def left_side(rows):
    return lax.broadcasted_iota(jnp.int32, (rows, LANES), 1) < BLOCK


def swap_matrix(swap):
    r = lax.broadcasted_iota(jnp.int32, (256, 256), 0)
    c = lax.broadcasted_iota(jnp.int32, (256, 256), 1)
    swap[...] = (c == (r % 16) * 16 + r // 16).astype(BF16)


def swapped(swap, parts):
    stacked = [jnp.concatenate(part, axis=0) for part in parts]
    return dot(swap[...], jnp.concatenate(stacked, axis=1)).astype(BF16)


def blocks_from_rows(tile, blocks, at, swap):
    for half in range(2):
        got = swapped(
            swap, [[tile(half, 16 * u + t) for t in range(16)] for u in range(2)]
        )
        for g in range(16):
            for u in range(2):
                blocks[at + 16 * half + g, 16 * u:16 * (u + 1), :] = (
                    got[16 * g:16 * (g + 1), u * LANES:(u + 1) * LANES]
                )


def tiles_from_rows(tile, tiles, at, swap):
    left = left_side(16)
    for half in range(2):
        for pair in range(2):
            parts = []
            for w in (2 * pair, 2 * pair + 1):
                part = []
                for t in range(8 * w, 8 * w + 8):
                    plain = tile(half, t)
                    turned = rotate(plain)
                    part += [jnp.where(left, plain, turned), jnp.where(left, turned, plain)]
                parts.append(part)
            got = swapped(swap, parts)
            for g in range(16):
                for u in range(2):
                    w = 2 * pair + u
                    tiles[at + 16 * half + g, 16 * w:16 * (w + 1), :] = (
                        got[16 * g:16 * (g + 1), u * LANES:(u + 1) * LANES]
                    )


def transposed_tiles(hats, flipped):
    r = lax.broadcasted_iota(jnp.int32, (BLOCK, LANES), 0)
    c = lax.broadcasted_iota(jnp.int32, (BLOCK, LANES), 1)
    pick = (c == 2 * (r % 32) + r // 32).astype(BF16)
    left = left_side(BLOCK)

    def body(p, carry):
        for inner in range(4):
            g = 8 * p + 2 * inner
            one, two = hats[g], hats[g + 1]
            stacked = jnp.concatenate([one, rotate(one), two, rotate(two)], axis=0)
            both = lax.dot_general(
                pick, stacked, (((1,), (1,)), ((), ())), preferred_element_type=F32
            ).astype(BF16)
            turned = rotate(both)
            flipped[g] = jnp.where(left, both, turned)
            flipped[g + 1] = jnp.where(left, turned, both)
        return carry

    lax.fori_loop(0, 4, body, 0)


def pair_flipped(p, order, flipped):
    return jnp.where(left_side(BLOCK), flipped[order[2 * p]], flipped[order[2 * p + 1]])


def pair_products(p, k, first, order, cols, blocks, tiles):
    left, wide = left_side(32), left_side(BLOCK)
    g1, g2 = order[2 * p], order[2 * p + 1]
    a1 = blocks[k * ROWS + g1]
    a2 = blocks[k * ROWS + g2]
    even = jnp.where(left, a1, rotate(a2))
    odd = jnp.where(left, rotate(a1), a2)
    lhs = jnp.concatenate([even, odd], axis=0)
    nil = jnp.zeros((BLOCK, LANES), BF16)
    p1 = tiles[jnp.clip(cols[k, g1] - first, 0, 3 * ROWS - 1)]
    p2 = tiles[jnp.clip(cols[k, g2] - first, 0, 3 * ROWS - 1)]
    rhs = jnp.concatenate([jnp.where(wide, p1, nil), jnp.where(wide, nil, p2)], axis=0)
    return dot(lhs, rhs).astype(BF16)


def pair_terms(outer, product):
    wide = left_side(BLOCK)
    nil = jnp.zeros((BLOCK, LANES), BF16)
    spread = jnp.concatenate(
        [jnp.where(wide, product, nil), jnp.where(wide, nil, product)], axis=0
    )
    return dot(outer, spread)


def split_pair(total):
    left = left_side(32)
    even, odd = total[:32], total[32:]
    return jnp.where(left, even, rotate(odd)), jnp.where(left, rotate(even), odd)


def invert_all(v):
    lanes = lax.broadcasted_iota(jnp.int32, (BLOCK, LANES), 1)
    sub = lax.broadcasted_iota(jnp.int32, (8, LANES), 0)
    slab_of = lambda k: 2 * (k // 16) + k % 2
    for k in range(BLOCK):
        q, sk, nxt = (k // 2) % 8, slab_of(k), slab_of(min(k + 1, BLOCK - 1))
        near = (k // 8) * 8
        index = (lanes // 8) * 8 + q
        row = jnp.take_along_axis(v[pl.ds(sk * BLOCK, BLOCK), :], index, axis=1)
        inverse = 1.0 / row[k:k + 1]
        scaled = row * inverse
        here = sub == k - near
        picked = lanes[:8] % 8 == q
        inverse = jnp.broadcast_to(inverse, (8, LANES))
        for s in [nxt] + [s for s in range(8) if s != nxt]:
            col = jnp.broadcast_to(v[pl.ds(s * BLOCK + k, 1), :], (8, LANES))
            for j in [near] + [j for j in range(0, BLOCK, 8) if j != near]:
                old = v[pl.ds(s * BLOCK + j, 8), :]
                part = scaled[j:j + 8]
                if j == near:
                    old = jnp.where(here, 0.0, old)
                    part = jnp.where(here, inverse, part)
                new = old - col * part
                if s == sk:
                    new = jnp.where(picked, part, new)
                v[pl.ds(s * BLOCK + j, 8), :] = new


def kernel(
    order, cols, a_hbm, p_hbm, coarse_ref, inverse_ref,
    a_flat, p_flat, halo, blocks, hats, tiles, flipped, swap, products,
    first_send, first_got, rest_send, rest_got, kept, whole, nat, v,
    a_sem, p_sem, halo_send, halo_recv, first_sem, rest_send_sem, rest_recv_sem,
):
    slab = lax.axis_index("slab")
    mirror = lax.axis_index("mirror")
    mirrors = lax.axis_size("mirror")
    partner = slab + 1 - 2 * (slab % 2)
    up = (mirror + 1) % mirrors
    down = (mirror + mirrors - 1) % mirrors
    others = ({"mirror": up}, {"mirror": down}, {"slab": partner})
    first_row = (slab * mirrors + mirror - 1) * ROWS

    own = pltpu.make_async_copy(p_hbm, p_flat, p_sem)
    own.start()
    loads = [
        pltpu.make_async_copy(a_hbm.at[k], a_flat.at[k], a_sem.at[k]) for k in range(KA)
    ]
    for load in loads:
        load.start()

    barrier = pltpu.get_barrier_semaphore()
    for other in others:
        pl.semaphore_signal(barrier, inc=1, device_id=other, device_id_type=MESH)
    swap_matrix(swap)
    pl.semaphore_wait(barrier, 3)

    halos = [
        pltpu.make_async_remote_copy(
            src_ref=p_hbm, dst_ref=halo.at[side], send_sem=halo_send.at[side],
            recv_sem=halo_recv.at[side], device_id=target, device_id_type=MESH,
        )
        for side, target in enumerate(({"mirror": up}, {"mirror": down}))
    ]
    for copy in halos:
        copy.start()

    def cut(half, t):
        return slice(16 * half, 16 * half + 16), slice(t * LANES, (t + 1) * LANES)

    own.wait()
    blocks_from_rows(lambda half, t: p_flat[cut(half, t)], hats, 0, swap)
    tiles_from_rows(lambda half, t: p_flat[cut(half, t)], tiles, ROWS, swap)
    loads[0].wait()
    blocks_from_rows(lambda half, t: a_flat[(0, *cut(half, t))], blocks, 0, swap)
    transposed_tiles(hats, flipped)

    args = (first_row, order, cols, blocks, tiles)

    def first_terms(p):
        return pair_terms(pair_flipped(p, order, flipped), pair_products(p, 0, *args))

    for p in range(PAIRS):
        first_send[p * BLOCK:(p + 1) * BLOCK, :] = first_terms(p).astype(BF16)
    first = pltpu.make_async_remote_copy(
        src_ref=first_send, dst_ref=first_got, send_sem=first_sem.at[0],
        recv_sem=first_sem.at[1], device_id={"slab": partner}, device_id_type=MESH,
    )
    first.start()
    for p in range(PAIRS):
        kept[p * BLOCK:(p + 1) * BLOCK, :] = first_terms(p + PAIRS)

    for k in range(1, KA):
        loads[k].wait()

    def rest_blocks(k, carry):
        blocks_from_rows(lambda half, t: a_flat[(k, *cut(half, t))], blocks, k * ROWS, swap)
        return carry

    lax.fori_loop(1, KA, rest_blocks, 0)

    first.wait()

    wide = left_side(BLOCK)

    def diagonal(i, carry):
        for inner in range(4):
            p = 4 * i + inner
            total = kept[rows_of(p, BLOCK), :] + first_got[rows_of(p, BLOCK), :].astype(F32)
            one, two = split_pair(total.astype(BF16))
            whole[2 * p] = one
            whole[2 * p + 1] = two
            at = pl.multiple_of(p * BLOCK, BLOCK)
            nat[pl.ds(at, 32, stride=2), :] = total[:32]
            nat[pl.ds(at + 1, 32, stride=2), :] = total[32:]
            plain = nat[rows_of(p, BLOCK), :]
            turned = jnp.concatenate([plain, plain], axis=0).T
            turned = jnp.where(wide, turned[:BLOCK], turned[BLOCK:])
            nat[rows_of(p, BLOCK), :] = 0.5 * (plain + turned)
            even = nat[pl.ds(at, 32, stride=2), :]
            odd = nat[pl.ds(at + 1, 32, stride=2), :]
            one, two = split_pair(jnp.concatenate([even, odd], axis=0))
            kept[rows_of(2 * p, TILES), :] = one
            kept[rows_of(2 * p + 1, TILES), :] = two
        return carry

    lax.fori_loop(0, PAIRS // 4, diagonal, 0)
    for tk in range(4):
        stacked = jnp.concatenate(
            [kept[pl.ds(b * TILES + tk * 8, 8), :] for b in range(HALF)], axis=0
        )
        v[pl.ds(tk * LANES, LANES), :] = stacked.T
    invert_all(v)
    for tk in range(4):
        stacked = v[pl.ds(tk * LANES, LANES), :].T
        for b in range(HALF):
            nat[pl.ds(b * TILES + tk * 8, 8), :] = stacked[b * 8:(b + 1) * 8]
    for t in range(TILES):
        inverse_ref[:, t * LANES:(t + 1) * LANES] = nat[pl.ds(t, HALF, stride=TILES), :]

    for side in range(2):
        halos[side].wait()

    def halo_tiles(side, carry):
        tiles_from_rows(
            lambda half, t: halo[(side, *cut(half, t))], tiles, 2 * ROWS * side, swap
        )
        return carry

    lax.fori_loop(0, 2, halo_tiles, 0)

    per = PAIRS // CHUNKS
    rest = KA - 1

    def multiply(p):
        for k in range(1, KA):
            products[k - 1] = pair_products(p, k, *args)

    def project(p, put):
        outer = pair_flipped(p, order, flipped)
        for k in range(1, KA):
            put(k - 1, pair_terms(outer, products[k - 1]))

    def put_out(p, k, term):
        rest_send[p // per, rows_of((p % per) * rest + k, BLOCK), :] = term.astype(BF16)

    def put_kept(p, k, term):
        kept[rows_of(p * rest + k, BLOCK), :] = term

    multiply(0)
    sends = []
    for chunk in range(CHUNKS):
        def rest_out(p, carry):
            project(p, lambda k, term: put_out(p, k, term))
            multiply(p + 1)
            return carry

        lax.fori_loop(chunk * per, (chunk + 1) * per, rest_out, 0)
        copy = pltpu.make_async_remote_copy(
            src_ref=rest_send.at[chunk], dst_ref=rest_got.at[chunk],
            send_sem=rest_send_sem.at[chunk], recv_sem=rest_recv_sem.at[chunk],
            device_id={"slab": partner}, device_id_type=MESH,
        )
        copy.start()
        sends.append(copy)

    def rest_kept(p, carry):
        project(p + PAIRS, lambda k, term: put_kept(p, k, term))
        multiply(p + PAIRS + 1)
        return carry

    lax.fori_loop(0, PAIRS - 1, rest_kept, 0)
    project(HALF - 1, lambda k, term: put_kept(PAIRS - 1, k, term))
    for chunk in range(CHUNKS):
        sends[chunk].wait()

        def add(p, carry):
            for k in range(1, KA):
                got = rest_got[p // per, rows_of((p % per) * rest + k - 1, BLOCK), :]
                total = kept[rows_of(p * rest + k - 1, BLOCK), :] + got.astype(F32)
                one, two = split_pair(total.astype(BF16))
                whole[k * HALF + 2 * p] = one
                whole[k * HALF + 2 * p + 1] = two
            return carry

        lax.fori_loop(chunk * per, (chunk + 1) * per, add, 0)

    def flatten(k, carry):
        got = swapped(
            swap,
            [[whole[k * HALF + c, 16 * u:16 * (u + 1), :] for c in range(HALF)] for u in range(2)],
        )
        for u in range(2):
            for t in range(16):
                at = (16 * u + t) * LANES
                coarse_ref[k, :, at:at + LANES] = (
                    got[16 * t:16 * (t + 1), u * LANES:(u + 1) * LANES]
                )
        return carry

    lax.fori_loop(0, KA, flatten, 0)


def on_device(a_blocks, a_cols, p_blocks, p_agg):
    mirrors = lax.axis_size("mirror")
    slab = lax.axis_index("slab")
    mine = ((p_agg // HALF) // mirrors) % 2 == slab % 2
    place = p_agg % HALF + HALF * mine.astype(jnp.int32)
    row = jnp.arange(ROWS, dtype=jnp.int32)
    order = jnp.sum(jnp.where(place[None, :] == row[:, None], row[None, :], 0), axis=1)

    vmem = lambda *shape: pltpu.VMEM(shape, F32)
    half = lambda *shape: pltpu.VMEM(shape, BF16)
    dma = pltpu.SemaphoreType.DMA
    coarse, inverse = pl.pallas_call(
        kernel,
        out_shape=(
            jax.ShapeDtypeStruct((KA, HALF, BLOCK * BLOCK), BF16),
            jax.ShapeDtypeStruct((HALF, BLOCK * BLOCK), F32),
        ),
        in_specs=[
            pl.BlockSpec(memory_space=pltpu.SMEM),
            pl.BlockSpec(memory_space=pltpu.SMEM),
            pl.BlockSpec(memory_space=pl.ANY),
            pl.BlockSpec(memory_space=pl.ANY),
        ],
        out_specs=(
            pl.BlockSpec(memory_space=pltpu.VMEM),
            pl.BlockSpec(memory_space=pltpu.VMEM),
        ),
        scratch_shapes=[
            half(KA, ROWS, BLOCK * BLOCK),
            half(ROWS, BLOCK * BLOCK),
            half(2, ROWS, BLOCK * BLOCK),
            half(KA * ROWS, TILES, LANES),
            half(ROWS, TILES, LANES),
            half(3 * ROWS, BLOCK, LANES),
            half(ROWS, BLOCK, LANES),
            half(256, 256),
            half(KA - 1, BLOCK, LANES),
            half(PAIRS * BLOCK, LANES),
            half(PAIRS * BLOCK, LANES),
            half(CHUNKS, PAIRS // CHUNKS * (KA - 1) * BLOCK, LANES),
            half(CHUNKS, PAIRS // CHUNKS * (KA - 1) * BLOCK, LANES),
            vmem(PAIRS * (KA - 1) * BLOCK, LANES),
            half(KA * HALF, TILES, LANES),
            vmem(PAIRS * BLOCK, LANES),
            vmem(4 * LANES, LANES),
            dma((KA,)), dma, dma((2,)), dma((2,)), dma((2,)), dma((CHUNKS,)), dma((CHUNKS,)),
        ],
        compiler_params=pltpu.CompilerParams(
            collective_id=0, has_side_effects=True, vmem_limit_bytes=56 * 2**20
        ),
    )(order, jnp.transpose(a_cols), jnp.transpose(a_blocks, (1, 0, 2)), p_blocks)
    return jnp.transpose(coarse, (1, 0, 2)), inverse


def solution(mesh):
    placed = (
        P(("slab", "mirror"), None, None),
        P(("slab", "mirror"), None),
        P(("slab", "mirror"), None),
        P(("slab", "mirror")),
    )
    return jax.shard_map(
        on_device,
        mesh=mesh,
        in_specs=placed,
        out_specs=(P(("slab", "mirror"), None, None), P(("slab", "mirror"), None)),
        check_vma=False,
    )
```

time: 51.1 us -> 32.5 us (0.64)
  Pallas kernels: 44.6 us -> 27.4 us
  other arithmetic: 2.01 us -> 1.31 us
  local copies, waits for them, and re-layouts: 3.58 us -> 2.92 us
    pallas_call x1, Pallas kernels: 44.6 us -> 27.4 us  [on_device(): pl.pallas_call(kernel, out_shape=(jax.ShapeDtypeStruct((KA, HALF, BLOCK *...]
    sub x1 -> x0, other arithmetic: 0.69 us -> none  [on_device(): local = a_cols - (device - 1) * ROWS]
    reshape x1 -> x0, local copies, waits for them, and re-layouts: 0.65 us -> none  [on_device(): jnp.sum(jnp.where(match[:, :, None], full[None], 0), axis=1).reshape(-1)]
where the time goes in v2:
time: 32.5 us; the launch traced here: 32.3 us
  Pallas kernels  27.4 us (84%)
  local copies, waits for them, and re-layouts  2.92 us (9%)
  other arithmetic  1.31 us (4%)
  between operations  0.66 us (2%)
    pallas_call x1, Pallas kernels, on_device(): pl.pallas_call(kernel, out_shape=(jax.ShapeDtypeStruct((KA, HALF, BLOCK *...  27.4 us
    unnamed x4, local copies, waits for them, and re-layouts  2.92 us
    add x1, other arithmetic, on_device(): place = p_agg % HALF + HALF * mine.astype(jnp.int32)  0.68 us

profile of v2, /device:TPU:1, one launch (start us, length us, event | category | flops | bytes accessed | tf_op | source)
XLA Modules:
  0.0 32.3 jit_solution(9624465166302564003)
XLA Ops:
  0.6 0.7 %fusion = s32[32]{0:T(128)S(1)} fusion(s32[32]{0:T(128)} %param.7, s32[]{:T(128)S(6)} %select_n.33), kind=kLoop, calls=%fused_computation.15 | loop fusion | flops 1536 | bytes 260 | tf_op jit(solution)/shard_map/add | solution.py:363
  1.3 0.6 %select_reduce_fusion.order = s32[32]{0:T(128)} fusion(s32[32]{0:T(128)S(1)} %fusion), kind=kLoop, calls=%fused_computation | loop fusion | flops 3040 | bytes 256 | tf_op jit(solution)/shard_map/reduce_sum | solution.py:365
  2.0 27.4 %shard_map.59 = (bf16[7,16,4096]{2,1,0:T(8,128)(2,1)}, f32[16,4096]{1,0:T(8,128)}) custom-call(s32[32]{0:T(128)} %select_reduce_fusion.order, s32[7,32]{1,0:T(8,128)} %bitcast.5, bf16[7,32,4096]{2,1,0:T(8,128)(2,1)} %bitcast.3, bf16[32,4096]{1,0:T(8,128)(2,1)} %p_hbm.1), custom_call_target="tpu_custom_call" | custom-call | tf_op jit(solution)/shard_map/pallas_call | solution.py:370
  29.4 0.0 copy-start
  29.4 2.2 %copy.8 = bf16[16,7,4096]{2,0,1:T(8,128)(2,1)} copy(bf16[16,7,4096]{2,0,1:T(8,128)(2,1)} %bitcast.4) | data formatting | bytes 1835008
  31.6 0.0 copy-done
  31.6 0.7 %copy.9 = f32[16,4096]{1,0:T(8,128)} copy(f32[16,4096]{1,0:T(8,128)S(1)} %copy-done) | data formatting | bytes 524288
Async XLA Ops:
  29.4 2.2 %copy-start = (f32[16,4096]{1,0:T(8,128)S(1)}, f32[16,4096]{1,0:T(8,128)}, u32[]{:S(2)}) copy-start(f32[16,4096]{1,0:T(8,128)} %get-tuple-element.9) | copy-start | bytes 786436

commit v3 on v2

--- a/solution.py
+++ b/solution.py
@@ -1,3 +1,5 @@
+import functools
+
 import jax
 import jax.numpy as jnp
 from jax import lax
@@ -133,11 +135,13 @@
     return jnp.where(left, even, rotate(odd)), jnp.where(left, rotate(even), odd)
 
 
-def invert_all(v):
+def invert_all(v, meanwhile):
     lanes = lax.broadcasted_iota(jnp.int32, (BLOCK, LANES), 1)
     sub = lax.broadcasted_iota(jnp.int32, (8, LANES), 0)
     slab_of = lambda k: 2 * (k // 16) + k % 2
     for k in range(BLOCK):
+        if k in meanwhile:
+            meanwhile[k]()
         q, sk, nxt = (k // 2) % 8, slab_of(k), slab_of(min(k + 1, BLOCK - 1))
         near = (k // 8) * 8
         index = (lanes // 8) * 8 + q
@@ -162,10 +166,10 @@
 
 
 def kernel(
-    order, cols, a_hbm, p_hbm, coarse_ref, inverse_ref,
-    a_flat, p_flat, halo, blocks, hats, tiles, flipped, swap, products,
+    order, cols_hbm, a_hbm, p_hbm, coarse_ref, inverse_ref,
+    cols, a_flat, p_flat, halo, blocks, hats, tiles, flipped, swap, products,
     first_send, first_got, rest_send, rest_got, kept, whole, nat, v,
-    a_sem, p_sem, halo_send, halo_recv, first_sem, rest_send_sem, rest_recv_sem,
+    cols_sem, a_sem, p_sem, halo_send, halo_recv, first_sem, rest_send_sem, rest_recv_sem,
 ):
     slab = lax.axis_index("slab")
     mirror = lax.axis_index("mirror")
@@ -178,6 +182,8 @@
 
     own = pltpu.make_async_copy(p_hbm, p_flat, p_sem)
     own.start()
+    index = pltpu.make_async_copy(cols_hbm, cols, cols_sem)
+    index.start()
     loads = [
         pltpu.make_async_copy(a_hbm.at[k], a_flat.at[k], a_sem.at[k]) for k in range(KA)
     ]
@@ -209,6 +215,7 @@
     loads[0].wait()
     blocks_from_rows(lambda half, t: a_flat[(0, *cut(half, t))], blocks, 0, swap)
     transposed_tiles(hats, flipped)
+    index.wait()
 
     args = (first_row, order, cols, blocks, tiles)
 
@@ -228,12 +235,11 @@
     for k in range(1, KA):
         loads[k].wait()
 
-    def rest_blocks(k, carry):
+    def rest_blocks(k):
         blocks_from_rows(lambda half, t: a_flat[(k, *cut(half, t))], blocks, k * ROWS, swap)
-        return carry
-
-    lax.fori_loop(1, KA, rest_blocks, 0)
-
+
+    for k in range(1, 4):
+        rest_blocks(k)
     first.wait()
 
     wide = left_side(BLOCK)
@@ -265,7 +271,17 @@
             [kept[pl.ds(b * TILES + tk * 8, 8), :] for b in range(HALF)], axis=0
         )
         v[pl.ds(tk * LANES, LANES), :] = stacked.T
-    invert_all(v)
+
+    def halo_tiles(side):
+        halos[side].wait()
+        tiles_from_rows(
+            lambda half, t: halo[(side, *cut(half, t))], tiles, 2 * ROWS * side, swap
+        )
+
+    meanwhile = {10 * k - 38: functools.partial(rest_blocks, k) for k in range(4, KA)}
+    meanwhile[38] = functools.partial(halo_tiles, 0)
+    meanwhile[50] = functools.partial(halo_tiles, 1)
+    invert_all(v, meanwhile)
     for tk in range(4):
         stacked = v[pl.ds(tk * LANES, LANES), :].T
         for b in range(HALF):
@@ -273,44 +289,33 @@
     for t in range(TILES):
         inverse_ref[:, t * LANES:(t + 1) * LANES] = nat[pl.ds(t, HALF, stride=TILES), :]
 
-    for side in range(2):
-        halos[side].wait()
-
-    def halo_tiles(side, carry):
-        tiles_from_rows(
-            lambda half, t: halo[(side, *cut(half, t))], tiles, 2 * ROWS * side, swap
-        )
-        return carry
-
-    lax.fori_loop(0, 2, halo_tiles, 0)
-
     per = PAIRS // CHUNKS
     rest = KA - 1
 
-    def multiply(p):
+    def multiply(p, side):
         for k in range(1, KA):
-            products[k - 1] = pair_products(p, k, *args)
-
-    def project(p, put):
+            products[side * rest + k - 1] = pair_products(p, k, *args)
+
+    def project(p, side, put):
         outer = pair_flipped(p, order, flipped)
-        for k in range(1, KA):
-            put(k - 1, pair_terms(outer, products[k - 1]))
-
-    def put_out(p, k, term):
-        rest_send[p // per, rows_of((p % per) * rest + k, BLOCK), :] = term.astype(BF16)
+        for k in range(rest):
+            put(k, pair_terms(outer, products[side * rest + k]))
 
     def put_kept(p, k, term):
         kept[rows_of(p * rest + k, BLOCK), :] = term
 
-    multiply(0)
+    for side in range(per):
+        multiply(side, side)
     sends = []
     for chunk in range(CHUNKS):
-        def rest_out(p, carry):
-            project(p, lambda k, term: put_out(p, k, term))
-            multiply(p + 1)
-            return carry
-
-        lax.fori_loop(chunk * per, (chunk + 1) * per, rest_out, 0)
+        for side in range(per):
+            def put_out(k, term):
+                at = (side * rest + k) * BLOCK
+                rest_send[chunk, at:at + BLOCK, :] = term.astype(BF16)
+
+            project(chunk * per + side, side, put_out)
+        for side in range(per):
+            multiply((chunk + 1) * per + side, side)
         copy = pltpu.make_async_remote_copy(
             src_ref=rest_send.at[chunk], dst_ref=rest_got.at[chunk],
             send_sem=rest_send_sem.at[chunk], recv_sem=rest_recv_sem.at[chunk],
@@ -319,13 +324,18 @@
         copy.start()
         sends.append(copy)
 
-    def rest_kept(p, carry):
-        project(p + PAIRS, lambda k, term: put_kept(p, k, term))
-        multiply(p + PAIRS + 1)
+    def rest_kept(i, carry):
+        for side in range(per):
+            p = i * per + side
+            project(p + PAIRS, side, functools.partial(put_kept, p))
+        for side in range(per):
+            multiply((i + 1) * per + side + PAIRS, side)
         return carry
 
-    lax.fori_loop(0, PAIRS - 1, rest_kept, 0)
-    project(HALF - 1, lambda k, term: put_kept(PAIRS - 1, k, term))
+    lax.fori_loop(0, CHUNKS - 1, rest_kept, 0)
+    for side in range(per):
+        p = PAIRS - per + side
+        project(p + PAIRS, side, functools.partial(put_kept, p))
     for chunk in range(CHUNKS):
         sends[chunk].wait()
 
@@ -340,7 +350,7 @@
 
         lax.fori_loop(chunk * per, (chunk + 1) * per, add, 0)
 
-    def flatten(k, carry):
+    for k in range(KA):
         got = swapped(
             swap,
             [[whole[k * HALF + c, 16 * u:16 * (u + 1), :] for c in range(HALF)] for u in range(2)],
@@ -351,18 +361,16 @@
                 coarse_ref[k, :, at:at + LANES] = (
                     got[16 * t:16 * (t + 1), u * LANES:(u + 1) * LANES]
                 )
-        return carry
-
-    lax.fori_loop(0, KA, flatten, 0)
 
 
 def on_device(a_blocks, a_cols, p_blocks, p_agg):
     mirrors = lax.axis_size("mirror")
     slab = lax.axis_index("slab")
-    mine = ((p_agg // HALF) // mirrors) % 2 == slab % 2
-    place = p_agg % HALF + HALF * mine.astype(jnp.int32)
     row = jnp.arange(ROWS, dtype=jnp.int32)
-    order = jnp.sum(jnp.where(place[None, :] == row[:, None], row[None, :], 0), axis=1)
+    device = slab * mirrors + lax.axis_index("mirror")
+    partner = (slab + 1 - 2 * (slab % 2)) * mirrors + lax.axis_index("mirror")
+    target = jnp.where(row < HALF, partner * HALF + row, device * HALF + row - HALF)
+    order = jnp.sum(jnp.where(p_agg[None, :] == target[:, None], row[None, :], 0), axis=1)
 
     vmem = lambda *shape: pltpu.VMEM(shape, F32)
     half = lambda *shape: pltpu.VMEM(shape, BF16)
@@ -375,15 +383,16 @@
         ),
         in_specs=[
             pl.BlockSpec(memory_space=pltpu.SMEM),
-            pl.BlockSpec(memory_space=pltpu.SMEM),
-            pl.BlockSpec(memory_space=pl.ANY),
-            pl.BlockSpec(memory_space=pl.ANY),
+            pl.BlockSpec(memory_space=pltpu.HBM),
+            pl.BlockSpec(memory_space=pltpu.HBM),
+            pl.BlockSpec(memory_space=pltpu.HBM),
         ],
         out_specs=(
             pl.BlockSpec(memory_space=pltpu.VMEM),
             pl.BlockSpec(memory_space=pltpu.VMEM),
         ),
         scratch_shapes=[
+            pltpu.SMEM((KA, ROWS), jnp.int32),
             half(KA, ROWS, BLOCK * BLOCK),
             half(ROWS, BLOCK * BLOCK),
             half(2, ROWS, BLOCK * BLOCK),
@@ -392,7 +401,7 @@
             half(3 * ROWS, BLOCK, LANES),
             half(ROWS, BLOCK, LANES),
             half(256, 256),
-            half(KA - 1, BLOCK, LANES),
+            half(PAIRS // CHUNKS * (KA - 1), BLOCK, LANES),
             half(PAIRS * BLOCK, LANES),
             half(PAIRS * BLOCK, LANES),
             half(CHUNKS, PAIRS // CHUNKS * (KA - 1) * BLOCK, LANES),
@@ -401,10 +410,10 @@
             half(KA * HALF, TILES, LANES),
             vmem(PAIRS * BLOCK, LANES),
             vmem(4 * LANES, LANES),
-            dma((KA,)), dma, dma((2,)), dma((2,)), dma((2,)), dma((CHUNKS,)), dma((CHUNKS,)),
+            dma, dma((KA,)), dma, dma((2,)), dma((2,)), dma((2,)), dma((CHUNKS,)), dma((CHUNKS,)),
         ],
         compiler_params=pltpu.CompilerParams(
-            collective_id=0, has_side_effects=True, vmem_limit_bytes=56 * 2**20
+            collective_id=0, has_side_effects=True, vmem_limit_bytes=51 * 2**20
         ),
     )(order, jnp.transpose(a_cols), jnp.transpose(a_blocks, (1, 0, 2)), p_blocks)
     return jnp.transpose(coarse, (1, 0, 2)), inverse

time: 32.5 us -> 27.3 us (0.84)
  Pallas kernels: 27.4 us -> 22.3 us
  other arithmetic: 1.31 us -> 0.84 us
  local copies, waits for them, and re-layouts: 2.92 us -> 3.26 us
    pallas_call x1, Pallas kernels: 27.4 us -> 22.3 us  [on_device(): pl.pallas_call(kernel, out_shape=(jax.ShapeDtypeStruct((KA, HALF, BLOCK *...]
    add x1 -> x0, other arithmetic: 0.68 us -> none  [on_device(): place = p_agg % HALF + HALF * mine.astype(jnp.int32)]
    unnamed x4 -> x6, local copies, waits for them, and re-layouts: 2.92 us -> 3.26 us
where the time goes in v3:
time: 27.3 us; the launch traced here: 27.1 us
  Pallas kernels  22.3 us (82%)
  local copies, waits for them, and re-layouts  3.26 us (12%)
  other arithmetic  0.84 us (3%)
  between operations  0.67 us (2%)
    pallas_call x1, Pallas kernels, on_device(): pl.pallas_call(kernel, out_shape=(jax.ShapeDtypeStruct((KA, HALF, BLOCK *...  22.3 us
    unnamed x6, local copies, waits for them, and re-layouts  3.26 us
    reduce_sum x1, other arithmetic, on_device(): jnp.sum(jnp.where(p_agg[None, :] == target[:, None], row[None, :], 0), ax...  0.84 us

profile of v3, /device:TPU:1, one launch (start us, length us, event | category | flops | bytes accessed | tf_op | source)
XLA Modules:
  0.0 27.1 jit_solution(6993960284925051733)
XLA Ops:
  0.7 0.8 %select_reduce_fusion.order = s32[32]{0:T(128)S(1)} fusion(s32[32]{0:T(128)} %param.7, s32[32]{0:T(128)S(1)} %compare_select_fusion), kind=kLoop, calls=%fused_computation | loop fusion | flops 3040 | bytes 384 | tf_op jit(solution)/shard_map/reduce_sum | solution.py:373
  1.5 0.0 copy-start
  1.5 0.9 %copy-done = bf16[32,4096]{1,0:T(8,128)(2,1)S(1)} copy-done((bf16[32,4096]{1,0:T(8,128)(2,1)S(1)}, bf16[32,4096]{1,0:T(8,128)(2,1)}, u32[]{:S(2)}) %copy-start) | copy-done | bytes 262168
  2.5 0.0 copy-start.1
  2.5 0.7 %copy-done.1 = s32[32,7]{0,1:T(8,128)S(1)} copy-done((s32[32,7]{0,1:T(8,128)S(1)}, s32[32,7]{0,1:T(8,128)}, u32[]{:S(2)}) %copy-start.1) | copy-done | bytes 920
  3.1 22.3 %shard_map.59 = (bf16[7,16,4096]{2,1,0:T(8,128)(2,1)S(1)}, f32[16,4096]{1,0:T(8,128)S(1)}) custom-call(s32[32]{0:T(128)S(1)} %select_reduce_fusion.order, s32[7,32]{1,0:T(8,128)S(1)} %bitcast.4, bf16[7,32,4096]{2,1,0:T(8,128)(2,1)} %bitcast.5, bf16[32,4096]{1,0:T(8,128)(2,1)S(1)} %copy-done), custom_call_target="tpu_custom_call" | custom-call | tf_op jit(solution)/shard_map/pallas_call | solution.py:378
  25.4 0.9 %copy.8 = bf16[16,7,4096]{2,0,1:T(8,128)(2,1)} copy(bf16[16,7,4096]{2,0,1:T(8,128)(2,1)S(1)} %bitcast.3) | data formatting | bytes 1835008
  26.4 0.7 %copy.9 = f32[16,4096]{1,0:T(8,128)} copy(f32[16,4096]{1,0:T(8,128)S(1)} %get-tuple-element.9) | data formatting | bytes 524288
  (1 shorter events, 0.0 us)
Async XLA Ops:
  1.5 1.0 %copy-start = (bf16[32,4096]{1,0:T(8,128)(2,1)S(1)}, bf16[32,4096]{1,0:T(8,128)(2,1)}, u32[]{:S(2)}) copy-start(bf16[32,4096]{1,0:T(8,128)(2,1)} %p_hbm.1) | copy-start | bytes 786436
  2.5 0.7 %copy-start.1 = (s32[32,7]{0,1:T(8,128)S(1)}, s32[32,7]{0,1:T(8,128)}, u32[]{:S(2)}) copy-start(s32[32,7]{0,1:T(8,128)} %param.5) | copy-start | bytes 2692
